TPU v7x, 256 devices: a whole 4x4x8 slice. The times are simulated.
256 devices in a mesh: seq: 32 (over y, z), tensor: 8 (over x, core).
Axes of the slice: x: 4, y: 4, z: 8, core: 2. Of those that a mesh axis runs over, the one named last changes fastest.
Arguments:
- hidden: bfloat16 [8192, 2048], P(('seq', 'tensor')), may hold values from -6 to 6
- attn_gain: float32 [2048], replicated, may hold values from 0.25 to 1.75
- attn_query: bfloat16 [2048, 2048], P(None, 'tensor'), may hold values from -0.015625 to 0.015625
- attn_key: bfloat16 [2048, 2048], P(None, 'tensor'), may hold values from -0.125 to 0.125
- attn_value: bfloat16 [2048, 2048], P(None, 'tensor'), may hold values from -0.125 to 0.125
- attn_out: bfloat16 [2048, 2048], P('tensor'), may hold values from -0.125 to 0.125
- ff_gain: float32 [2048], replicated, may hold values from 0.25 to 1.75
- ff_gate: bfloat16 [2048, 5120], P(None, 'tensor'), may hold values from -0.125 to 0.125
- ff_up: bfloat16 [2048, 5120], P(None, 'tensor'), may hold values from -0.125 to 0.125
- ff_down: bfloat16 [5120, 2048], P('tensor'), may hold values from -0.078125 to 0.078125
- final_gain: float32 [2048], replicated, may hold values from 0.25 to 1.75
- embedding: bfloat16 [32128, 2048], P('seq', 'tensor'), may hold values from -0.375 to 0.375
- rel_weight: float32 [32, 32], P(None, 'tensor'), may hold values from -6 to 6
- bucket_table: int32 [2048], replicated, may hold values from 0 to 31
- prefix_kv: bfloat16 [2, 32, 256, 2048], P(None, 'seq', None, 'tensor'), may hold values from -1600 to 1600, as said below
- node_lengths: int32 [32], replicated, may hold values from 1 to 256, 3072 in all
- group_branch: int32 [24], replicated, may hold values from 0 to 6
- node_slot: int32 [32], replicated, may hold values from 0 to 31, each once
- request_group: int32 [32], replicated, may hold values from 0 to 23
Outputs:
- hidden_out: bfloat16 [8192, 2048], P(('seq', 'tensor'))
- last_rms: float32 [32], replicated
- top_logit: float32 [32], replicated
Inputs may be any that keep to these rules, and one draw needn't show every extreme that they name: `prefix_kv`: finite entries.
All inputs are finite; a program needn't handle non-finite values.
Results may differ from a plain program's by a relative error of at most 0.018.
The roundings to bfloat16 on the way count: a program that leaves them out, or rounds other values in their place, can miss the bound.
Values may be sent and summed in bfloat16 or wider, within the bound.
A program may use at most 192 MiB of HBM per device.

v0:
```python
import functools

import jax
import jax.numpy as jnp
from jax import lax
from jax.experimental import pallas as pl
from jax.experimental.pallas import tpu as pltpu
from jax.sharding import PartitionSpec as P

MESH = pl.DeviceIdType.MESH
BRANCHES = 7
EPS = 1e-06
MASKED = -1e30
F32 = jnp.float32
BF16 = jnp.bfloat16
NT = (((1,), (1,)), ((), ()))


def remote(src, dst, send_sem, recv_sem, **device):
    return pltpu.make_async_remote_copy(
        src_ref=src, dst_ref=dst, send_sem=send_sem, recv_sem=recv_sem, device_id=device, device_id_type=MESH
    )


def dot(a, b):
    return jnp.dot(a, b, preferred_element_type=F32)


def rms_scale(values, gain):
    mean_square = jnp.mean(values * values, axis=-1, keepdims=True)
    return (values * lax.rsqrt(mean_square + EPS) * gain).astype(BF16)


def kernel(
    ns,
    nt,
    node_lengths,
    group_branch,
    node_slot,
    request_group,
    rel_weight,
    hidden,
    attn_gain,
    ff_gain,
    final_gain,
    bucket_table,
    kv_in,
    wq_in,
    wk_in,
    wv_in,
    wo_in,
    wg_in,
    wu_in,
    wd_in,
    emb_in,
    out,
    misc,
    wq,
    wk,
    wv,
    wo,
    wg,
    wu,
    wd,
    emb,
    full1,
    full2,
    slots,
    kv_send,
    path_kv,
    bias,
    query,
    own_key,
    own_value,
    attn,
    inner_rows,
    half_send1,
    half_recv1,
    part_send1,
    part_recv1,
    half_send2,
    half_recv2,
    part_send2,
    part_recv2,
    own_sum,
    last_send,
    last_mine,
    last_all,
    logit_send,
    logit_all,
    top_t,
    top_s,
    wsem,
    ag_send,
    ag_recv,
    rs_send,
    rs_recv,
    seq_send,
    seq_recv,
    tail_send,
    tail_recv,
):
    nx = nt // 2
    nz = 8 if ns % 8 == 0 else ns
    ny = ns // nz
    me_s = lax.axis_index("seq")
    me_t = lax.axis_index("tensor")
    x, core = me_t // 2, me_t % 2
    y, z = me_s // nz, me_s % nz
    sibling = me_t + 1 - 2 * core
    rows, width = hidden.shape
    suf = rows * nt
    heads = rel_weight.shape[1]
    cols = wq.shape[1]
    chunk = kv_in.shape[1]
    cap = chunk * ns // 2

    def seq_peer(k):
        return ((y + k // nz) % ny) * nz + (z + k % nz) % nz

    def seq_from(k):
        return ((y + ny - k // nz) % ny) * nz + (z + nz - k % nz) % nz

    weights = [(wq_in, wq), (wk_in, wk), (wv_in, wv), (wo_in, wo), (wg_in, wg), (wu_in, wu), (wd_in, wd), (emb_in, emb)]
    loads = [pltpu.make_async_copy(a, b, wsem.at[i]) for i, (a, b) in enumerate(weights)]
    own_slot = pltpu.make_async_copy(kv_in.at[me_s], slots.at[me_s], wsem.at[len(weights)])
    own_slot.start()
    for load in loads:
        load.start()

    barrier = pltpu.get_barrier_semaphore()

    @pl.loop(1, ns)
    def _(k):
        pl.semaphore_signal(barrier, inc=1, device_id={"seq": seq_peer(k)}, device_id_type=MESH)

    for k in range(1, nt):
        pl.semaphore_signal(barrier, inc=1, device_id={"tensor": (me_t + k) % nt}, device_id_type=MESH)

    full1[me_t] = rms_scale(hidden[...].astype(F32), attn_gain[...])
    pl.semaphore_wait(barrier, ns - 1 + nt - 1)

    @pl.loop(1, ns)
    def _(k):
        peer = seq_peer(k)
        remote(kv_in.at[peer], slots.at[me_s], seq_send.at[0, k], seq_recv.at[0, me_s], seq=peer).start()

    def gather_start(buf, phase):
        copies = [remote(buf.at[me_t], buf.at[me_t], ag_send.at[phase, 0], ag_recv.at[phase, me_t], tensor=sibling)]
        for k in range(1, nx):
            peer = ((x + k) % nx) * 2 + core
            copies.append(remote(buf.at[me_t], buf.at[me_t], ag_send.at[phase, k], ag_recv.at[phase, me_t], tensor=peer))
        for copy in copies:
            copy.start()
        return copies

    def gather_finish(buf, phase, copies):
        for k in range(1, nx):
            block = ((x + nx - k) % nx) * 2 + core
            remote(buf.at[block], buf.at[block], ag_send.at[phase, nx], ag_recv.at[phase, block], tensor=sibling).wait_recv()
            copy = remote(
                buf.at[block], buf.at[block], ag_send.at[phase, nx - 1 + k], ag_recv.at[phase, block], tensor=sibling
            )
            copy.start()
            copies.append(copy)
        for k in range(nx):
            block = ((x + nx - k) % nx) * 2 + 1 - core
            remote(buf.at[block], buf.at[block], ag_send.at[phase, nx], ag_recv.at[phase, block], tensor=sibling).wait_recv()
        for copy in copies:
            copy.wait_send()
        return buf[...].reshape(suf, width)

    copies = gather_start(full1, 0)

    def path_of(request):
        group = request_group[request]
        return 0, 1 + group_branch[group], 1 + BRANCHES + group

    nodes = path_of(me_s)
    lengths = [node_lengths[n] for n in nodes]
    base = lengths[0] + lengths[1] + lengths[2]
    starts = [0, lengths[0], lengths[0] + lengths[1], base]

    rels = bucket_table.shape[1]
    table = jnp.broadcast_to(bucket_table[...], (8, rels))
    sub = lax.broadcasted_iota(jnp.int32, (8, 1), 0)
    head_bias = jnp.zeros((8, rels), F32)
    for b in range(rel_weight.shape[0]):
        column = jnp.zeros((8, 1), F32)
        for h in range(heads):
            column = jnp.where(sub == h, rel_weight[b, h], column)
        head_bias = jnp.where(table == b, column, head_bias)
    half = suf // 2
    span = 2 * suf
    for part in range(4):
        first = rels // 2 - suf + 1 + starts[part] - base
        slab = pltpu.roll(head_bias, rels - first, 1)[:, :span]
        for h in range(heads):
            spread = jnp.broadcast_to(slab[h : h + 1, :], (half, span))
            turned = pltpu.roll(spread, span - half + 1, 1, stride=1, stride_axis=0)
            bias[h, part] = turned[:, : span - half]

    @pl.loop(1, ns)
    def _(k):
        peer = seq_from(k)
        remote(kv_in.at[peer], slots.at[peer], seq_send.at[0, k], seq_recv.at[0, peer], seq=peer).wait_recv()

    own_slot.wait()

    @pl.loop(1, ns)
    def _(k):
        peer = seq_peer(k)
        for level, node in enumerate(path_of(peer)):
            kv_send[k, level] = slots[node_slot[node]]
        remote(kv_send.at[k], path_kv.at[:, me_s], seq_send.at[1, k], seq_recv.at[1, me_s], seq=peer).start()

    for level, node in enumerate(nodes):
        path_kv[level, me_s] = slots[node_slot[node]]

    all_rows = gather_finish(full1, 0, copies)
    for i, (weight, result) in enumerate(((wq, query), (wk, own_key), (wv, own_value))):
        loads[i].wait()
        result[...] = dot(all_rows, weight[...]).astype(BF16)

    @pl.loop(1, ns)
    def _(k):
        peer = seq_from(k)
        remote(kv_send.at[k], path_kv.at[:, peer], seq_send.at[1, k], seq_recv.at[1, peer], seq=peer).wait_recv()

    lane = lax.broadcasted_iota(jnp.int32, (1, cap), 1)
    penalty = [jnp.where(lane < lengths[level], 0.0, MASKED) for level in range(3)]
    pair_lane = lax.broadcasted_iota(jnp.int32, (1, 128), 1)
    per_pair = 128 // (cols // heads)
    half_chunks = ns // 2
    for pair in range(cols // 128):
        at = slice(pair * 128, pair * 128 + 128)
        keys = [path_kv[level, :half_chunks, :, at].reshape(cap, 128) for level in range(3)] + [own_key[:, at]]
        values = [path_kv[level, half_chunks:, :, at].reshape(cap, 128) for level in range(3)] + [own_value[:, at]]
        for block in range(2):
            pair_query = query[block * half : block * half + half, at]
            merged = None
            for e in range(per_pair):
                h = pair * per_pair + e
                mine = pair_lane // (128 // per_pair) == e
                head_query = jnp.where(mine, pair_query, jnp.zeros((), BF16))
                scores = []
                for part in range(4):
                    score = lax.dot_general(head_query, keys[part], NT, preferred_element_type=F32)
                    score = score + bias[h, part, :, half * (1 - block) : half * (1 - block) + suf]
                    scores.append(score + penalty[part] if part < 3 else score)
                peak = jnp.max(jnp.maximum(jnp.maximum(scores[0], scores[1]), jnp.maximum(scores[2], scores[3])), axis=1, keepdims=True)
                total = None
                summed = None
                for part in range(4):
                    prob = jnp.exp(scores[part] - peak)
                    total = prob if total is None else total + prob
                    term = dot(prob.astype(BF16), values[part])
                    summed = term if summed is None else summed + term
                head_out = summed / jnp.sum(total, axis=1, keepdims=True)
                merged = head_out if merged is None else jnp.where(mine, head_out, merged)
            merged = merged.astype(BF16)
            for r in range(half // rows):
                attn[block * (half // rows) + r, :, at] = merged[r * rows : r * rows + rows]

    def scatter_sum(left, weight, half_send, half_recv, part_send, part_recv, phase):
        def product(parity):
            picked = jnp.concatenate([left[2 * i + parity] for i in range(nx)], axis=0)
            return dot(picked, weight[...]).reshape(nx, rows, width)

        half_send[...] = product(1 - core).astype(BF16)
        over = remote(half_send, half_recv, rs_send.at[phase, 0], rs_recv.at[phase, nx], tensor=sibling)
        over.start()
        own_sum[...] = product(core)
        over.wait_recv()
        sent = [over]
        for k in range(1, nx):
            dest = (x + k) % nx
            part_send[k] = (own_sum[dest] + half_recv[dest].astype(F32)).astype(BF16)
            copy = remote(
                part_send.at[k], part_recv.at[x], rs_send.at[phase, k], rs_recv.at[phase, x], tensor=dest * 2 + core
            )
            copy.start()
            sent.append(copy)
        total = own_sum[x] + half_recv[x].astype(F32)
        for k in range(1, nx):
            source = (x + nx - k) % nx
            remote(
                part_send.at[k], part_recv.at[source], rs_send.at[phase, k], rs_recv.at[phase, source], tensor=sibling
            ).wait_recv()
            total = total + part_recv[source].astype(F32)
        for copy in sent:
            copy.wait_send()
        return total

    loads[3].wait()
    summed = scatter_sum(attn, wo, half_send1, half_recv1, part_send1, part_recv1, 0)
    mid = (hidden[...].astype(F32) + summed).astype(BF16).astype(F32)
    full2[me_t] = rms_scale(mid, ff_gain[...])
    copies = gather_start(full2, 1)
    all_rows = gather_finish(full2, 1, copies)
    loads[4].wait()
    loads[5].wait()
    gate = dot(all_rows, wg[...])
    up = dot(all_rows, wu[...])
    inner = (jax.nn.gelu(gate, approximate=True) * up).astype(BF16)
    inner_rows[...] = inner.reshape(nt, rows, inner.shape[1])
    loads[6].wait()
    total = scatter_sum(inner_rows, wd, half_send2, half_recv2, part_send2, part_recv2, 1)
    result = (mid + total).astype(BF16)
    out[...] = result

    last = result[rows - 1 : rows].astype(F32)
    mean_square = jnp.mean(last * last, axis=-1, keepdims=True)
    rms = jnp.broadcast_to(jnp.sqrt(mean_square), (1, 128))
    final = (last * lax.rsqrt(mean_square + EPS) * final_gain[...]).astype(BF16).astype(F32)
    for t in range(nt):
        last_send[t] = jnp.concatenate([final[:, t * cols : t * cols + cols], rms], axis=1)

    @pl.when(me_t == nt - 1)
    def _():
        sends = [
            remote(last_send.at[t], last_mine, tail_send.at[0, t], tail_recv.at[0, 0], tensor=t) for t in range(nt - 1)
        ]
        for send in sends:
            send.start()
        last_mine[...] = last_send[nt - 1]
        for send in sends:
            send.wait_send()

    @pl.when(me_t != nt - 1)
    def _():
        remote(last_send.at[0], last_mine, tail_send.at[0, 0], tail_recv.at[0, 0], tensor=sibling).wait_recv()

    @pl.loop(1, ns)
    def _(k):
        remote(last_mine, last_all.at[me_s], seq_send.at[2, k], seq_recv.at[2, me_s], seq=seq_peer(k)).start()

    last_all[me_s] = last_mine[...]
    loads[7].wait()

    @pl.loop(1, ns)
    def _(k):
        peer = seq_from(k)
        remote(last_mine, last_all.at[peer], seq_send.at[2, k], seq_recv.at[2, peer], seq=peer).wait_recv()

    lasts = last_all[...].reshape(ns, cols + 128)
    rms_all = lasts[:, cols:]
    vocab = emb.shape[0]
    logits = lax.dot_general(lasts[:, :cols].astype(BF16), emb[...], NT, preferred_element_type=F32)
    per = 128 * pl.cdiv(pl.cdiv(vocab, nt), 128)
    logits = jnp.concatenate([logits, jnp.full((ns, per * nt - vocab), MASKED, F32)], axis=1)
    for t in range(nt):
        logit_send[t] = logits[:, t * per : t * per + per]
    sends = []
    for k in range(1, nt):
        peer = (me_t + k) % nt
        send = remote(logit_send.at[peer], logit_all.at[me_t], tail_send.at[1, k], tail_recv.at[1, me_t], tensor=peer)
        send.start()
        sends.append(send)
    logit = logit_send[me_t]
    for k in range(1, nt):
        peer = (me_t + nt - k) % nt
        remote(logit_send.at[peer], logit_all.at[peer], tail_send.at[1, k], tail_recv.at[1, peer], tensor=peer).wait_recv()
        logit = logit + logit_all[peer]
    highest = jnp.max(logit, axis=1, keepdims=True)
    diagonal = lax.broadcasted_iota(jnp.int32, (ns, 128), 0) == lax.broadcasted_iota(jnp.int32, (ns, 128), 1)
    top_t[me_t] = jnp.max(jnp.where(diagonal, highest, 2 * nt * MASKED), axis=0, keepdims=True)
    for k in range(1, nt):
        peer = (me_t + k) % nt
        send = remote(top_t.at[me_t], top_t.at[me_t], tail_send.at[2, k], tail_recv.at[2, me_t], tensor=peer)
        send.start()
        sends.append(send)
    top = top_t[me_t]
    for k in range(1, nt):
        peer = (me_t + nt - k) % nt
        remote(top_t.at[peer], top_t.at[peer], tail_send.at[2, k], tail_recv.at[2, peer], tensor=peer).wait_recv()
        top = jnp.maximum(top, top_t[peer])
    top_s[me_s] = top

    @pl.loop(1, ns)
    def _(k):
        remote(top_s.at[me_s], top_s.at[me_s], seq_send.at[3, k], seq_recv.at[3, me_s], seq=seq_peer(k)).start()

    last_rms = jnp.sum(jnp.where(diagonal, rms_all, 0.0), axis=0, keepdims=True)

    @pl.loop(1, ns)
    def _(k):
        peer = seq_from(k)
        remote(top_s.at[peer], top_s.at[peer], seq_send.at[3, k], seq_recv.at[3, peer], seq=peer).wait_recv()

    top = jnp.max(top_s[...].reshape(ns, 128), axis=0, keepdims=True)
    misc[...] = jnp.concatenate([last_rms, top, jnp.zeros((6, 128), F32)], axis=0)

    for send in sends:
        send.wait_send()

    @pl.loop(1, ns)
    def _(k):
        peer = seq_peer(k)
        remote(kv_in.at[peer], slots.at[me_s], seq_send.at[0, k], seq_recv.at[0, me_s], seq=peer).wait_send()
        remote(kv_send.at[k], path_kv.at[:, me_s], seq_send.at[1, k], seq_recv.at[1, me_s], seq=peer).wait_send()
        remote(last_mine, last_all.at[me_s], seq_send.at[2, k], seq_recv.at[2, me_s], seq=peer).wait_send()
        remote(top_s.at[me_s], top_s.at[me_s], seq_send.at[3, k], seq_recv.at[3, me_s], seq=peer).wait_send()


def per_device(
    hidden,
    attn_gain,
    attn_query,
    attn_key,
    attn_value,
    attn_out,
    ff_gain,
    ff_gate,
    ff_up,
    ff_down,
    final_gain,
    embedding,
    rel_weight,
    bucket_table,
    prefix_kv,
    node_lengths,
    group_branch,
    node_slot,
    request_group,
):
    ns = lax.axis_size("seq")
    nt = lax.axis_size("tensor")
    nx = nt // 2
    rows, width = hidden.shape
    suf = rows * nt
    heads = rel_weight.shape[1]
    cols = attn_query.shape[1]
    cap = prefix_kv.shape[2]
    chunk = 2 * cap // ns
    per = 128 * pl.cdiv(pl.cdiv(embedding.shape[0], nt), 128)
    kv_chunks = prefix_kv.reshape(ns, chunk, cols)
    smem = pl.BlockSpec(memory_space=pltpu.SMEM)
    vmem = pl.BlockSpec(memory_space=pltpu.VMEM)
    hbm = pl.BlockSpec(memory_space=pl.ANY)
    weights = (attn_query, attn_key, attn_value, attn_out, ff_gate, ff_up, ff_down, embedding)
    dma = pltpu.SemaphoreType.DMA
    result, misc = pl.pallas_call(
        functools.partial(kernel, ns, nt),
        out_shape=(jax.ShapeDtypeStruct((rows, width), BF16), jax.ShapeDtypeStruct((8, 128), F32)),
        in_specs=[smem] * 5 + [vmem] * 5 + [hbm] * 9,
        out_specs=(vmem, vmem),
        scratch_shapes=[pltpu.VMEM(w.shape, BF16) for w in weights]
        + [
            pltpu.VMEM((nt, rows, width), BF16),
            pltpu.VMEM((nt, rows, width), BF16),
            pltpu.VMEM((ns, chunk, cols), BF16),
            pltpu.VMEM((ns, 3, chunk, cols), BF16),
            pltpu.VMEM((3, ns, chunk, cols), BF16),
            pltpu.VMEM((heads, 4, suf // 2, suf + suf // 2), F32),
            pltpu.VMEM((suf, cols), BF16),
            pltpu.VMEM((suf, cols), BF16),
            pltpu.VMEM((suf, cols), BF16),
            pltpu.VMEM((nt, rows, cols), BF16),
            pltpu.VMEM((nt, rows, ff_down.shape[0]), BF16),
        ]
        + [pltpu.VMEM((nx, rows, width), BF16) for _ in range(8)]
        + [
            pltpu.VMEM((nx, rows, width), F32),
            pltpu.VMEM((nt, 1, cols + 128), F32),
            pltpu.VMEM((1, cols + 128), F32),
            pltpu.VMEM((ns, 1, cols + 128), F32),
            pltpu.VMEM((nt, ns, per), F32),
            pltpu.VMEM((nt, ns, per), F32),
            pltpu.VMEM((nt, 1, 128), F32),
            pltpu.VMEM((ns, 1, 128), F32),
            dma((len(weights) + 1,)),
            dma((2, 2 * nx)),
            dma((2, nt)),
            dma((2, nx)),
            dma((2, nx + 1)),
            dma((4, ns)),
            dma((4, ns)),
            dma((3, nt)),
            dma((3, nt)),
        ],
        compiler_params=pltpu.CompilerParams(collective_id=0, has_side_effects=True, vmem_limit_bytes=60 << 20),
        name="layer",
    )(
        node_lengths,
        group_branch,
        node_slot,
        request_group,
        rel_weight,
        hidden,
        attn_gain.reshape(1, -1),
        ff_gain.reshape(1, -1),
        final_gain.reshape(1, -1),
        bucket_table.reshape(1, -1),
        kv_chunks,
        *weights,
    )
    return result, misc[0, :ns], misc[1, :ns]


def solution(mesh):
    return jax.shard_map(
        per_device,
        mesh=mesh,
        in_specs=(
            P(("seq", "tensor"), None),
            P(),
            P(None, "tensor"),
            P(None, "tensor"),
            P(None, "tensor"),
            P("tensor", None),
            P(),
            P(None, "tensor"),
            P(None, "tensor"),
            P("tensor", None),
            P(),
            P("seq", "tensor"),
            P(None, "tensor"),
            P(),
            P(None, "seq", None, "tensor"),
            P(),
            P(),
            P(),
            P(),
        ),
        out_specs=(P(("seq", "tensor"), None), P(), P()),
        check_vma=False,
    )
```

profile of v0, /device:TPU:1, one launch (start us, length us, event | category | flops | bytes accessed | tf_op | source)
XLA Modules:
  0.0 105.7 jit_solution(880430932424437008)
XLA Ops:
  0.6 1.4 %copy.22.rel_weight = f32[32,4]{1,0:T(8,128)} copy(f32[32,4]{0,1:T(4,128)} %param.31) | data formatting | bytes 1024 | tf_op args[12]
  2.0 100.9 %layer.1 = (bf16[32,2048]{1,0:T(8,128)(2,1)}, f32[8,128]{1,0:T(8,128)}) custom-call(s32[32]{0:T(128)} %node_lengths.1, s32[24]{0:T(128)} %group_branch.1, s32[32]{0:T(128)} %node_slot.1, s32[32]{0:T(128)} %request_group.1, f32[32,4]{1,0:T(8,128)} %copy.22.rel_weight, bf16[32,2048]{1,0:T(8,128)(2,1)} %hidden.1, f32[1,2048]{1,0:T(1,128)} %bitcast.10, ...), custom_call_target="tpu_custom_call" | custom-call | tf_op jit(solution)/shard_map/layer/pallas_call | solution.py:443
  102.9 1.3 %slice_bitcast_fusion = (f32[32]{0:T(128)}, f32[32]{0:T(128)}) fusion(f32[8,128]{1,0:T(8,128)} %get-tuple-element.6), kind=kLoop, calls=%fused_computation | loop fusion | bytes 512 | tf_op jit(solution)/shard_map/squeeze | solution.py:498
  104.1 1.6 %copy.24 = bf16[32,2048]{1,0:T(8,128)(2,1)} copy(bf16[32,2048]{1,0:T(8,128)(2,1)} %get-tuple-element.12) | data formatting | bytes 262144
where the time goes:
time: 106 us
  Pallas kernels  101 us (95%)
  local copies, waits for them, and re-layouts  4.2 us (4%)
    pallas_call x1, Pallas kernels, per_device(): pl.pallas_call(functools.partial(kernel, ns, nt), out_shape=(jax.ShapeDty...  101 us
    unnamed x2, local copies, waits for them, and re-layouts  2.93 us

commit v1 on v0

--- a/solution.py
+++ b/solution.py
@@ -84,7 +84,8 @@
     part_recv2,
     own_sum,
     last_send,
-    last_mine,
+    row_out,
+    row_in,
     last_all,
     logit_send,
     logit_all,
@@ -262,7 +263,116 @@
             for r in range(half // rows):
                 attn[block * (half // rows) + r, :, at] = merged[r * rows : r * rows + rows]
 
-    def scatter_sum(left, weight, half_send, half_recv, part_send, part_recv, phase):
+    def row_send(row, phase):
+        row_out[phase] = row
+        for k in range(1, nt):
+            peer = (me_t + k) % nt
+            send = remote(
+                row_out.at[phase], row_in.at[phase, me_t], tail_send.at[phase, k], tail_recv.at[phase, me_t], tensor=peer
+            )
+            send.start()
+            sends.append(send)
+
+    def row_sum(phase):
+        row = row_out[phase]
+        for k in range(1, nt):
+            peer = (me_t + nt - k) % nt
+            remote(
+                row_out.at[phase], row_in.at[phase, peer], tail_send.at[phase, k], tail_recv.at[phase, peer], tensor=peer
+            ).wait_recv()
+            row = row + row_in[phase, peer]
+        return row
+
+    sends = []
+    is_last = me_t == nt - 1
+
+    def last_projected():
+        row = dot(attn[nt - 1, rows - 16 : rows], wo[...])[15:16]
+        row_send(row + jnp.where(is_last, hidden[rows - 1 : rows].astype(F32), 0.0), 0)
+
+    def last_inner():
+        row = row_sum(0).astype(BF16).astype(F32)
+        left = jnp.broadcast_to(rms_scale(row, ff_gain[...]).astype(F32), (16, width)).astype(BF16)
+        inner = (jax.nn.gelu(dot(left, wg[...]), approximate=True) * dot(left, wu[...])).astype(BF16)
+        row_send(dot(inner, wd[...])[0:1] + jnp.where(is_last, row, 0.0), 1)
+
+    def last_final():
+        last = row_sum(1).astype(BF16).astype(F32)
+        mean_square = jnp.mean(last * last, axis=-1, keepdims=True)
+        rms = jnp.broadcast_to(jnp.sqrt(mean_square), (1, 128))
+        final = (last * lax.rsqrt(mean_square + EPS) * final_gain[...]).astype(BF16).astype(F32)
+        for t in range(nt):
+            last_send[t] = jnp.concatenate([final[:, t * cols : t * cols + cols], rms], axis=1)
+
+        @pl.loop(1, ns)
+        def _(k):
+            remote(
+                last_send.at[me_t], last_all.at[me_s], seq_send.at[2, k], seq_recv.at[2, me_s], seq=seq_peer(k)
+            ).start()
+
+        last_all[me_s] = last_send[me_t]
+
+    per = logit_send.shape[2]
+    diagonal = lax.broadcasted_iota(jnp.int32, (ns, 128), 0) == lax.broadcasted_iota(jnp.int32, (ns, 128), 1)
+
+    def last_logits():
+        @pl.loop(1, ns)
+        def _(k):
+            peer = seq_from(k)
+            remote(
+                last_send.at[me_t], last_all.at[peer], seq_send.at[2, k], seq_recv.at[2, peer], seq=peer
+            ).wait_recv()
+
+        lasts = last_all[...].reshape(ns, cols + 128)
+        vocab = emb.shape[0]
+        logits = lax.dot_general(lasts[:, :cols].astype(BF16), emb[...], NT, preferred_element_type=F32)
+        logits = jnp.concatenate([logits, jnp.full((ns, per * nt - vocab), MASKED, F32)], axis=1)
+        for t in range(nt):
+            logit_send[t] = logits[:, t * per : t * per + per]
+        for k in range(1, nt):
+            peer = (me_t + k) % nt
+            send = remote(logit_send.at[peer], logit_all.at[me_t], tail_send.at[2, k], tail_recv.at[2, me_t], tensor=peer)
+            send.start()
+            sends.append(send)
+        misc[0:1] = jnp.sum(jnp.where(diagonal, lasts[:, cols:], 0.0), axis=0, keepdims=True)
+
+    def top_of_words():
+        logit = logit_send[me_t]
+        for k in range(1, nt):
+            peer = (me_t + nt - k) % nt
+            remote(
+                logit_send.at[peer], logit_all.at[peer], tail_send.at[2, k], tail_recv.at[2, peer], tensor=peer
+            ).wait_recv()
+            logit = logit + logit_all[peer]
+        highest = jnp.max(logit, axis=1, keepdims=True)
+        top_t[me_t] = jnp.max(jnp.where(diagonal, highest, 2 * nt * MASKED), axis=0, keepdims=True)
+        for k in range(1, nt):
+            peer = (me_t + k) % nt
+            send = remote(top_t.at[me_t], top_t.at[me_t], tail_send.at[3, k], tail_recv.at[3, me_t], tensor=peer)
+            send.start()
+            sends.append(send)
+
+    def top_of_group():
+        top = top_t[me_t]
+        for k in range(1, nt):
+            peer = (me_t + nt - k) % nt
+            remote(top_t.at[peer], top_t.at[peer], tail_send.at[3, k], tail_recv.at[3, peer], tensor=peer).wait_recv()
+            top = jnp.maximum(top, top_t[peer])
+        top_s[me_s] = top
+
+        @pl.loop(1, ns)
+        def _(k):
+            remote(top_s.at[me_s], top_s.at[me_s], seq_send.at[3, k], seq_recv.at[3, me_s], seq=seq_peer(k)).start()
+
+    def top_of_all():
+        @pl.loop(1, ns)
+        def _(k):
+            peer = seq_from(k)
+            remote(top_s.at[peer], top_s.at[peer], seq_send.at[3, k], seq_recv.at[3, peer], seq=peer).wait_recv()
+
+        misc[1:2] = jnp.max(top_s[...].reshape(ns, 128), axis=0, keepdims=True)
+
+    def scatter_sum(left, weight, half_send, half_recv, part_send, part_recv, phase, early, late):
         def product(parity):
             picked = jnp.concatenate([left[2 * i + parity] for i in range(nx)], axis=0)
             return dot(picked, weight[...]).reshape(nx, rows, width)
@@ -271,6 +381,7 @@
         over = remote(half_send, half_recv, rs_send.at[phase, 0], rs_recv.at[phase, nx], tensor=sibling)
         over.start()
         own_sum[...] = product(core)
+        early()
         over.wait_recv()
         sent = [over]
         for k in range(1, nx):
@@ -282,6 +393,7 @@
             copy.start()
             sent.append(copy)
         total = own_sum[x] + half_recv[x].astype(F32)
+        late()
         for k in range(1, nx):
             source = (x + nx - k) % nx
             remote(
@@ -292,105 +404,26 @@
             copy.wait_send()
         return total
 
-    loads[3].wait()
-    summed = scatter_sum(attn, wo, half_send1, half_recv1, part_send1, part_recv1, 0)
+    for i in range(3, 8):
+        loads[i].wait()
+    last_projected()
+    summed = scatter_sum(attn, wo, half_send1, half_recv1, part_send1, part_recv1, 0, lambda: None, last_inner)
     mid = (hidden[...].astype(F32) + summed).astype(BF16).astype(F32)
     full2[me_t] = rms_scale(mid, ff_gain[...])
     copies = gather_start(full2, 1)
+    last_final()
     all_rows = gather_finish(full2, 1, copies)
-    loads[4].wait()
-    loads[5].wait()
+    last_logits()
     gate = dot(all_rows, wg[...])
     up = dot(all_rows, wu[...])
     inner = (jax.nn.gelu(gate, approximate=True) * up).astype(BF16)
     inner_rows[...] = inner.reshape(nt, rows, inner.shape[1])
-    loads[6].wait()
-    total = scatter_sum(inner_rows, wd, half_send2, half_recv2, part_send2, part_recv2, 1)
+    top_of_words()
+    total = scatter_sum(inner_rows, wd, half_send2, half_recv2, part_send2, part_recv2, 1, top_of_group, lambda: None)
     result = (mid + total).astype(BF16)
     out[...] = result
 
-    last = result[rows - 1 : rows].astype(F32)
-    mean_square = jnp.mean(last * last, axis=-1, keepdims=True)
-    rms = jnp.broadcast_to(jnp.sqrt(mean_square), (1, 128))
-    final = (last * lax.rsqrt(mean_square + EPS) * final_gain[...]).astype(BF16).astype(F32)
-    for t in range(nt):
-        last_send[t] = jnp.concatenate([final[:, t * cols : t * cols + cols], rms], axis=1)
-
-    @pl.when(me_t == nt - 1)
-    def _():
-        sends = [
-            remote(last_send.at[t], last_mine, tail_send.at[0, t], tail_recv.at[0, 0], tensor=t) for t in range(nt - 1)
-        ]
-        for send in sends:
-            send.start()
-        last_mine[...] = last_send[nt - 1]
-        for send in sends:
-            send.wait_send()
-
-    @pl.when(me_t != nt - 1)
-    def _():
-        remote(last_send.at[0], last_mine, tail_send.at[0, 0], tail_recv.at[0, 0], tensor=sibling).wait_recv()
-
-    @pl.loop(1, ns)
-    def _(k):
-        remote(last_mine, last_all.at[me_s], seq_send.at[2, k], seq_recv.at[2, me_s], seq=seq_peer(k)).start()
-
-    last_all[me_s] = last_mine[...]
-    loads[7].wait()
-
-    @pl.loop(1, ns)
-    def _(k):
-        peer = seq_from(k)
-        remote(last_mine, last_all.at[peer], seq_send.at[2, k], seq_recv.at[2, peer], seq=peer).wait_recv()
-
-    lasts = last_all[...].reshape(ns, cols + 128)
-    rms_all = lasts[:, cols:]
-    vocab = emb.shape[0]
-    logits = lax.dot_general(lasts[:, :cols].astype(BF16), emb[...], NT, preferred_element_type=F32)
-    per = 128 * pl.cdiv(pl.cdiv(vocab, nt), 128)
-    logits = jnp.concatenate([logits, jnp.full((ns, per * nt - vocab), MASKED, F32)], axis=1)
-    for t in range(nt):
-        logit_send[t] = logits[:, t * per : t * per + per]
-    sends = []
-    for k in range(1, nt):
-        peer = (me_t + k) % nt
-        send = remote(logit_send.at[peer], logit_all.at[me_t], tail_send.at[1, k], tail_recv.at[1, me_t], tensor=peer)
-        send.start()
-        sends.append(send)
-    logit = logit_send[me_t]
-    for k in range(1, nt):
-        peer = (me_t + nt - k) % nt
-        remote(logit_send.at[peer], logit_all.at[peer], tail_send.at[1, k], tail_recv.at[1, peer], tensor=peer).wait_recv()
-        logit = logit + logit_all[peer]
-    highest = jnp.max(logit, axis=1, keepdims=True)
-    diagonal = lax.broadcasted_iota(jnp.int32, (ns, 128), 0) == lax.broadcasted_iota(jnp.int32, (ns, 128), 1)
-    top_t[me_t] = jnp.max(jnp.where(diagonal, highest, 2 * nt * MASKED), axis=0, keepdims=True)
-    for k in range(1, nt):
-        peer = (me_t + k) % nt
-        send = remote(top_t.at[me_t], top_t.at[me_t], tail_send.at[2, k], tail_recv.at[2, me_t], tensor=peer)
-        send.start()
-        sends.append(send)
-    top = top_t[me_t]
-    for k in range(1, nt):
-        peer = (me_t + nt - k) % nt
-        remote(top_t.at[peer], top_t.at[peer], tail_send.at[2, k], tail_recv.at[2, peer], tensor=peer).wait_recv()
-        top = jnp.maximum(top, top_t[peer])
-    top_s[me_s] = top
-
-    @pl.loop(1, ns)
-    def _(k):
-        remote(top_s.at[me_s], top_s.at[me_s], seq_send.at[3, k], seq_recv.at[3, me_s], seq=seq_peer(k)).start()
-
-    last_rms = jnp.sum(jnp.where(diagonal, rms_all, 0.0), axis=0, keepdims=True)
-
-    @pl.loop(1, ns)
-    def _(k):
-        peer = seq_from(k)
-        remote(top_s.at[peer], top_s.at[peer], seq_send.at[3, k], seq_recv.at[3, peer], seq=peer).wait_recv()
-
-    top = jnp.max(top_s[...].reshape(ns, 128), axis=0, keepdims=True)
-    misc[...] = jnp.concatenate([last_rms, top, jnp.zeros((6, 128), F32)], axis=0)
-
+    top_of_all()
     for send in sends:
         send.wait_send()
 
@@ -399,7 +432,7 @@
         peer = seq_peer(k)
         remote(kv_in.at[peer], slots.at[me_s], seq_send.at[0, k], seq_recv.at[0, me_s], seq=peer).wait_send()
         remote(kv_send.at[k], path_kv.at[:, me_s], seq_send.at[1, k], seq_recv.at[1, me_s], seq=peer).wait_send()
-        remote(last_mine, last_all.at[me_s], seq_send.at[2, k], seq_recv.at[2, me_s], seq=peer).wait_send()
+        remote(last_send.at[me_t], last_all.at[me_s], seq_send.at[2, k], seq_recv.at[2, me_s], seq=peer).wait_send()
         remote(top_s.at[me_s], top_s.at[me_s], seq_send.at[3, k], seq_recv.at[3, me_s], seq=peer).wait_send()
 
 
@@ -463,7 +496,8 @@
         + [
             pltpu.VMEM((nx, rows, width), F32),
             pltpu.VMEM((nt, 1, cols + 128), F32),
-            pltpu.VMEM((1, cols + 128), F32),
+            pltpu.VMEM((2, 1, width), F32),
+            pltpu.VMEM((2, nt, 1, width), F32),
             pltpu.VMEM((ns, 1, cols + 128), F32),
             pltpu.VMEM((nt, ns, per), F32),
             pltpu.VMEM((nt, ns, per), F32),
@@ -476,8 +510,8 @@
             dma((2, nx + 1)),
             dma((4, ns)),
             dma((4, ns)),
-            dma((3, nt)),
-            dma((3, nt)),
+            dma((4, nt)),
+            dma((4, nt)),
         ],
         compiler_params=pltpu.CompilerParams(collective_id=0, has_side_effects=True, vmem_limit_bytes=60 << 20),
         name="layer",

time: 106 us -> 90.7 us (0.86)
  Pallas kernels: 101 us -> 85.6 us
    pallas_call x1, Pallas kernels: 101 us -> 85.6 us  [per_device(): pl.pallas_call(functools.partial(kernel, ns, nt), out_shape=(jax.ShapeDty...]
where the time goes in v1:
time: 90.7 us; the launch traced here: 90.5 us
  Pallas kernels  85.6 us (94%)
  local copies, waits for them, and re-layouts  4.2 us (5%)
    pallas_call x1, Pallas kernels, per_device(): pl.pallas_call(functools.partial(kernel, ns, nt), out_shape=(jax.ShapeDty...  85.6 us
    unnamed x2, local copies, waits for them, and re-layouts  2.93 us

profile of v1, /device:TPU:1, one launch (start us, length us, event | category | flops | bytes accessed | tf_op | source)
XLA Modules:
  0.0 90.5 jit_solution(10206631127042561472)
XLA Ops:
  0.6 1.4 %copy.22.rel_weight = f32[32,4]{1,0:T(8,128)} copy(f32[32,4]{0,1:T(4,128)} %param.31) | data formatting | bytes 1024 | tf_op args[12]
  2.0 85.6 %layer.1 = (bf16[32,2048]{1,0:T(8,128)(2,1)}, f32[8,128]{1,0:T(8,128)}) custom-call(s32[32]{0:T(128)} %node_lengths.1, s32[24]{0:T(128)} %group_branch.1, s32[32]{0:T(128)} %node_slot.1, s32[32]{0:T(128)} %request_group.1, f32[32,4]{1,0:T(8,128)} %copy.22.rel_weight, bf16[32,2048]{1,0:T(8,128)(2,1)} %hidden.1, f32[1,2048]{1,0:T(1,128)} %bitcast.10, ...), custom_call_target="tpu_custom_call" | custom-call | tf_op jit(solution)/shard_map/layer/pallas_call | solution.py:476
  87.6 1.3 %slice_bitcast_fusion = (f32[32]{0:T(128)}, f32[32]{0:T(128)}) fusion(f32[8,128]{1,0:T(8,128)} %get-tuple-element.6), kind=kLoop, calls=%fused_computation | loop fusion | bytes 512 | tf_op jit(solution)/shard_map/squeeze | solution.py:532
  88.9 1.6 %copy.24 = bf16[32,2048]{1,0:T(8,128)(2,1)} copy(bf16[32,2048]{1,0:T(8,128)(2,1)} %get-tuple-element.12) | data formatting | bytes 262144

commit v2 on v1

--- a/solution.py
+++ b/solution.py
@@ -67,6 +67,7 @@
     full2,
     slots,
     kv_send,
+    kv_column,
     path_kv,
     bias,
     query,
@@ -98,6 +99,10 @@
     rs_recv,
     seq_send,
     seq_recv,
+    z_send,
+    z_recv,
+    y_send,
+    y_recv,
     tail_send,
     tail_recv,
 ):
@@ -111,7 +116,7 @@
     sibling = me_t + 1 - 2 * core
     rows, width = hidden.shape
     suf = rows * nt
-    heads = rel_weight.shape[1]
+    heads, buckets = rel_weight.shape
     cols = wq.shape[1]
     chunk = kv_in.shape[1]
     cap = chunk * ns // 2
@@ -186,10 +191,10 @@
     table = jnp.broadcast_to(bucket_table[...], (8, rels))
     sub = lax.broadcasted_iota(jnp.int32, (8, 1), 0)
     head_bias = jnp.zeros((8, rels), F32)
-    for b in range(rel_weight.shape[0]):
+    for b in range(buckets):
         column = jnp.zeros((8, 1), F32)
         for h in range(heads):
-            column = jnp.where(sub == h, rel_weight[b, h], column)
+            column = jnp.where(sub == h, rel_weight[h, b], column)
         head_bias = jnp.where(table == b, column, head_bias)
     half = suf // 2
     span = 2 * suf
@@ -208,25 +213,87 @@
 
     own_slot.wait()
 
-    @pl.loop(1, ns)
-    def _(k):
-        peer = seq_peer(k)
-        for level, node in enumerate(path_of(peer)):
-            kv_send[k, level] = slots[node_slot[node]]
-        remote(kv_send.at[k], path_kv.at[:, me_s], seq_send.at[1, k], seq_recv.at[1, me_s], seq=peer).start()
-
-    for level, node in enumerate(nodes):
-        path_kv[level, me_s] = slots[node_slot[node]]
+    def column_chunks(column, to):
+        to[0] = slots[node_slot[0]]
+        for row in range(ny):
+            branch, lowest = path_of(row * nz + column)[1:]
+            to[1 + 2 * row] = slots[node_slot[branch]]
+            to[2 + 2 * row] = slots[node_slot[lowest]]
+
+    def z_step(i):
+        return (i // 2 + 1) * (1 - 2 * (i % 2))
+
+    def over_z(i):
+        column = (z + nz + z_step(i)) % nz
+        return remote(
+            kv_send.at[column], kv_column.at[z], z_send.at[i], z_recv.at[z], seq=y * nz + column
+        )
+
+    @pl.loop(0, nz - 1)
+    def _(i):
+        column = (z + nz + z_step(i)) % nz
+        column_chunks(column, kv_send.at[column])
+        over_z(i).start()
+
+    def over_y(k, column):
+        row = (y + k) % ny
+        at = y * nz + column
+        root = remote(
+            kv_column.at[column, 0],
+            path_kv.at[0, at],
+            y_send.at[0, k, column],
+            y_recv.at[0, at],
+            seq=row * nz + z,
+        )
+        below = remote(
+            kv_column.at[column, pl.ds(1 + 2 * row, 2)],
+            path_kv.at[pl.ds(1, 2), at],
+            y_send.at[1, k, column],
+            y_recv.at[1, at],
+            seq=row * nz + z,
+        )
+        return root, below
+
+    def pass_on(column):
+        for k in range(1, ny):
+            for copy in over_y(k, column):
+                copy.start()
+        at = y * nz + column
+        path_kv[0, at] = kv_column[column, 0]
+        path_kv[1, at] = kv_column[column, 1 + 2 * y]
+        path_kv[2, at] = kv_column[column, 2 + 2 * y]
+
+    column_chunks(z, kv_column.at[z])
+    pass_on(z)
 
     all_rows = gather_finish(full1, 0, copies)
     for i, (weight, result) in enumerate(((wq, query), (wk, own_key), (wv, own_value))):
         loads[i].wait()
         result[...] = dot(all_rows, weight[...]).astype(BF16)
 
-    @pl.loop(1, ns)
-    def _(k):
-        peer = seq_from(k)
-        remote(kv_send.at[k], path_kv.at[:, peer], seq_send.at[1, k], seq_recv.at[1, peer], seq=peer).wait_recv()
+    @pl.loop(0, nz - 1)
+    def _(i):
+        column = (z + nz - z_step(i)) % nz
+        remote(
+            kv_send.at[column], kv_column.at[column], z_send.at[i], z_recv.at[column], seq=y * nz + column
+        ).wait_recv()
+        pass_on(column)
+
+    @pl.loop(0, nz)
+    def _(column):
+        for k in range(1, ny):
+            row = (y + ny - k) % ny
+            at = row * nz + column
+            remote(
+                kv_column.at[column, 0], path_kv.at[0, at], y_send.at[0, k, column], y_recv.at[0, at], seq=row * nz + z
+            ).wait_recv()
+            remote(
+                kv_column.at[column, pl.ds(1, 2)],
+                path_kv.at[pl.ds(1, 2), at],
+                y_send.at[1, k, column],
+                y_recv.at[1, at],
+                seq=row * nz + z,
+            ).wait_recv()
 
     lane = lax.broadcasted_iota(jnp.int32, (1, cap), 1)
     penalty = [jnp.where(lane < lengths[level], 0.0, MASKED) for level in range(3)]
@@ -307,7 +374,7 @@
         @pl.loop(1, ns)
         def _(k):
             remote(
-                last_send.at[me_t], last_all.at[me_s], seq_send.at[2, k], seq_recv.at[2, me_s], seq=seq_peer(k)
+                last_send.at[me_t], last_all.at[me_s], seq_send.at[1, k], seq_recv.at[1, me_s], seq=seq_peer(k)
             ).start()
 
         last_all[me_s] = last_send[me_t]
@@ -320,7 +387,7 @@
         def _(k):
             peer = seq_from(k)
             remote(
-                last_send.at[me_t], last_all.at[peer], seq_send.at[2, k], seq_recv.at[2, peer], seq=peer
+                last_send.at[me_t], last_all.at[peer], seq_send.at[1, k], seq_recv.at[1, peer], seq=peer
             ).wait_recv()
 
         lasts = last_all[...].reshape(ns, cols + 128)
@@ -362,13 +429,13 @@
 
         @pl.loop(1, ns)
         def _(k):
-            remote(top_s.at[me_s], top_s.at[me_s], seq_send.at[3, k], seq_recv.at[3, me_s], seq=seq_peer(k)).start()
+            remote(top_s.at[me_s], top_s.at[me_s], seq_send.at[2, k], seq_recv.at[2, me_s], seq=seq_peer(k)).start()
 
     def top_of_all():
         @pl.loop(1, ns)
         def _(k):
             peer = seq_from(k)
-            remote(top_s.at[peer], top_s.at[peer], seq_send.at[3, k], seq_recv.at[3, peer], seq=peer).wait_recv()
+            remote(top_s.at[peer], top_s.at[peer], seq_send.at[2, k], seq_recv.at[2, peer], seq=peer).wait_recv()
 
         misc[1:2] = jnp.max(top_s[...].reshape(ns, 128), axis=0, keepdims=True)
 
@@ -431,9 +498,18 @@
     def _(k):
         peer = seq_peer(k)
         remote(kv_in.at[peer], slots.at[me_s], seq_send.at[0, k], seq_recv.at[0, me_s], seq=peer).wait_send()
-        remote(kv_send.at[k], path_kv.at[:, me_s], seq_send.at[1, k], seq_recv.at[1, me_s], seq=peer).wait_send()
-        remote(last_send.at[me_t], last_all.at[me_s], seq_send.at[2, k], seq_recv.at[2, me_s], seq=peer).wait_send()
-        remote(top_s.at[me_s], top_s.at[me_s], seq_send.at[3, k], seq_recv.at[3, me_s], seq=peer).wait_send()
+        remote(last_send.at[me_t], last_all.at[me_s], seq_send.at[1, k], seq_recv.at[1, me_s], seq=peer).wait_send()
+        remote(top_s.at[me_s], top_s.at[me_s], seq_send.at[2, k], seq_recv.at[2, me_s], seq=peer).wait_send()
+
+    @pl.loop(0, nz - 1)
+    def _(i):
+        over_z(i).wait_send()
+
+    @pl.loop(0, nz)
+    def _(column):
+        for k in range(1, ny):
+            for copy in over_y(k, column):
+                copy.wait_send()
 
 
 def per_device(
@@ -460,6 +536,8 @@
     ns = lax.axis_size("seq")
     nt = lax.axis_size("tensor")
     nx = nt // 2
+    nz = 8 if ns % 8 == 0 else ns
+    ny = ns // nz
     rows, width = hidden.shape
     suf = rows * nt
     heads = rel_weight.shape[1]
@@ -483,7 +561,8 @@
             pltpu.VMEM((nt, rows, width), BF16),
             pltpu.VMEM((nt, rows, width), BF16),
             pltpu.VMEM((ns, chunk, cols), BF16),
-            pltpu.VMEM((ns, 3, chunk, cols), BF16),
+            pltpu.VMEM((nz, 1 + 2 * ny, chunk, cols), BF16),
+            pltpu.VMEM((nz, 1 + 2 * ny, chunk, cols), BF16),
             pltpu.VMEM((3, ns, chunk, cols), BF16),
             pltpu.VMEM((heads, 4, suf // 2, suf + suf // 2), F32),
             pltpu.VMEM((suf, cols), BF16),
@@ -508,8 +587,12 @@
             dma((2, nt)),
             dma((2, nx)),
             dma((2, nx + 1)),
-            dma((4, ns)),
-            dma((4, ns)),
+            dma((3, ns)),
+            dma((3, ns)),
+            dma((nz - 1,)),
+            dma((nz,)),
+            dma((2, ny, nz)),
+            dma((2, ns)),
             dma((4, nt)),
             dma((4, nt)),
         ],
@@ -520,7 +603,7 @@
         group_branch,
         node_slot,
         request_group,
-        rel_weight,
+        rel_weight.T,
         hidden,
         attn_gain.reshape(1, -1),
         ff_gain.reshape(1, -1),

time: 90.7 us -> 91 us (level); the launches traced: 90.5 us -> 89.4 us
  local copies, waits for them, and re-layouts: 4.2 us -> 2.83 us
    unnamed x2 -> x1, local copies, waits for them, and re-layouts: 2.93 us -> 1.57 us
where the time goes in v2:
time: 91 us; the launch traced here: 89.4 us
  Pallas kernels  85.9 us (94%)
  local copies, waits for them, and re-layouts  2.83 us (3%)
    pallas_call x1, Pallas kernels, per_device(): pl.pallas_call(functools.partial(kernel, ns, nt), out_shape=(jax.ShapeDty...  85.9 us

profile of v2, /device:TPU:1, one launch (start us, length us, event | category | flops | bytes accessed | tf_op | source)
XLA Modules:
  0.0 89.4 jit_solution(15314095979097407592)
XLA Ops:
  0.6 85.9 %layer.1 = (bf16[32,2048]{1,0:T(8,128)(2,1)}, f32[8,128]{1,0:T(8,128)}) custom-call(s32[32]{0:T(128)} %node_lengths.1, s32[24]{0:T(128)} %group_branch.1, s32[32]{0:T(128)} %node_slot.1, s32[32]{0:T(128)} %request_group.1, f32[4,32]{1,0:T(4,128)} %bitcast.15, bf16[32,2048]{1,0:T(8,128)(2,1)} %hidden.1, f32[1,2048]{1,0:T(1,128)} %bitcast.11, ...), custom_call_target="tpu_custom_call" | custom-call | tf_op jit(solution)/shard_map/layer/pallas_call | solution.py:554
  86.5 1.3 %slice_bitcast_fusion = (f32[32]{0:T(128)}, f32[32]{0:T(128)}) fusion(f32[8,128]{1,0:T(8,128)} %get-tuple-element.6), kind=kLoop, calls=%fused_computation | loop fusion | bytes 512 | tf_op jit(solution)/shard_map/squeeze | solution.py:615
  87.8 1.6 %copy.23 = bf16[32,2048]{1,0:T(8,128)(2,1)} copy(bf16[32,2048]{1,0:T(8,128)(2,1)} %get-tuple-element.12) | data formatting | bytes 262144

commit v3 on v1

--- a/solution.py
+++ b/solution.py
@@ -67,6 +67,7 @@
     full2,
     slots,
     kv_send,
+    path_root,
     path_kv,
     bias,
     query,
@@ -98,6 +99,10 @@
     rs_recv,
     seq_send,
     seq_recv,
+    z_send,
+    z_recv,
+    y_send,
+    y_recv,
     tail_send,
     tail_recv,
 ):
@@ -111,7 +116,7 @@
     sibling = me_t + 1 - 2 * core
     rows, width = hidden.shape
     suf = rows * nt
-    heads = rel_weight.shape[1]
+    heads, buckets = rel_weight.shape
     cols = wq.shape[1]
     chunk = kv_in.shape[1]
     cap = chunk * ns // 2
@@ -186,10 +191,10 @@
     table = jnp.broadcast_to(bucket_table[...], (8, rels))
     sub = lax.broadcasted_iota(jnp.int32, (8, 1), 0)
     head_bias = jnp.zeros((8, rels), F32)
-    for b in range(rel_weight.shape[0]):
+    for b in range(buckets):
         column = jnp.zeros((8, 1), F32)
         for h in range(heads):
-            column = jnp.where(sub == h, rel_weight[b, h], column)
+            column = jnp.where(sub == h, rel_weight[h, b], column)
         head_bias = jnp.where(table == b, column, head_bias)
     half = suf // 2
     span = 2 * suf
@@ -208,15 +213,35 @@
 
     own_slot.wait()
 
+    path_root[me_s] = slots[node_slot[0]]
+
+    def root_z(k):
+        to = y * nz + (z + k) % nz
+        return remote(path_root.at[me_s], path_root.at[me_s], z_send.at[k], z_recv.at[z], seq=to)
+
+    def root_y(k):
+        row = path_root.at[pl.ds(y * nz, nz)]
+        return remote(row, row, y_send.at[k], y_recv.at[y], seq=((y + k) % ny) * nz + z)
+
+    for k in range(1, nz):
+        root_z(k).start()
+
     @pl.loop(1, ns)
     def _(k):
         peer = seq_peer(k)
-        for level, node in enumerate(path_of(peer)):
+        for level, node in enumerate(path_of(peer)[1:]):
             kv_send[k, level] = slots[node_slot[node]]
         remote(kv_send.at[k], path_kv.at[:, me_s], seq_send.at[1, k], seq_recv.at[1, me_s], seq=peer).start()
 
-    for level, node in enumerate(nodes):
+    for level, node in enumerate(nodes[1:]):
         path_kv[level, me_s] = slots[node_slot[node]]
+
+    for k in range(1, nz):
+        column = (z + nz - k) % nz
+        at = y * nz + column
+        remote(path_root.at[at], path_root.at[at], z_send.at[k], z_recv.at[column], seq=at).wait_recv()
+    for k in range(1, ny):
+        root_y(k).start()
 
     all_rows = gather_finish(full1, 0, copies)
     for i, (weight, result) in enumerate(((wq, query), (wk, own_key), (wv, own_value))):
@@ -227,6 +252,11 @@
     def _(k):
         peer = seq_from(k)
         remote(kv_send.at[k], path_kv.at[:, peer], seq_send.at[1, k], seq_recv.at[1, peer], seq=peer).wait_recv()
+
+    for k in range(1, ny):
+        row = (y + ny - k) % ny
+        chunks = path_root.at[pl.ds(row * nz, nz)]
+        remote(chunks, chunks, y_send.at[k], y_recv.at[row], seq=row * nz + z).wait_recv()
 
     lane = lax.broadcasted_iota(jnp.int32, (1, cap), 1)
     penalty = [jnp.where(lane < lengths[level], 0.0, MASKED) for level in range(3)]
@@ -235,8 +265,9 @@
     half_chunks = ns // 2
     for pair in range(cols // 128):
         at = slice(pair * 128, pair * 128 + 128)
-        keys = [path_kv[level, :half_chunks, :, at].reshape(cap, 128) for level in range(3)] + [own_key[:, at]]
-        values = [path_kv[level, half_chunks:, :, at].reshape(cap, 128) for level in range(3)] + [own_value[:, at]]
+        paths = (path_root, path_kv.at[0], path_kv.at[1])
+        keys = [path[:half_chunks, :, at].reshape(cap, 128) for path in paths] + [own_key[:, at]]
+        values = [path[half_chunks:, :, at].reshape(cap, 128) for path in paths] + [own_value[:, at]]
         for block in range(2):
             pair_query = query[block * half : block * half + half, at]
             merged = None
@@ -435,6 +466,11 @@
         remote(last_send.at[me_t], last_all.at[me_s], seq_send.at[2, k], seq_recv.at[2, me_s], seq=peer).wait_send()
         remote(top_s.at[me_s], top_s.at[me_s], seq_send.at[3, k], seq_recv.at[3, me_s], seq=peer).wait_send()
 
+    for k in range(1, nz):
+        root_z(k).wait_send()
+    for k in range(1, ny):
+        root_y(k).wait_send()
+
 
 def per_device(
     hidden,
@@ -460,6 +496,8 @@
     ns = lax.axis_size("seq")
     nt = lax.axis_size("tensor")
     nx = nt // 2
+    nz = 8 if ns % 8 == 0 else ns
+    ny = ns // nz
     rows, width = hidden.shape
     suf = rows * nt
     heads = rel_weight.shape[1]
@@ -483,8 +521,9 @@
             pltpu.VMEM((nt, rows, width), BF16),
             pltpu.VMEM((nt, rows, width), BF16),
             pltpu.VMEM((ns, chunk, cols), BF16),
-            pltpu.VMEM((ns, 3, chunk, cols), BF16),
-            pltpu.VMEM((3, ns, chunk, cols), BF16),
+            pltpu.VMEM((ns, 2, chunk, cols), BF16),
+            pltpu.VMEM((ns, chunk, cols), BF16),
+            pltpu.VMEM((2, ns, chunk, cols), BF16),
             pltpu.VMEM((heads, 4, suf // 2, suf + suf // 2), F32),
             pltpu.VMEM((suf, cols), BF16),
             pltpu.VMEM((suf, cols), BF16),
@@ -510,6 +549,10 @@
             dma((2, nx + 1)),
             dma((4, ns)),
             dma((4, ns)),
+            dma((nz,)),
+            dma((nz,)),
+            dma((ny,)),
+            dma((ny,)),
             dma((4, nt)),
             dma((4, nt)),
         ],
@@ -520,7 +563,7 @@
         group_branch,
         node_slot,
         request_group,
-        rel_weight,
+        rel_weight.T,
         hidden,
         attn_gain.reshape(1, -1),
         ff_gain.reshape(1, -1),

time: 90.7 us -> 85.5 us (0.943)
  Pallas kernels: 85.6 us -> 81.7 us
  local copies, waits for them, and re-layouts: 4.2 us -> 2.83 us
    pallas_call x1, Pallas kernels: 85.6 us -> 81.7 us  [per_device(): pl.pallas_call(functools.partial(kernel, ns, nt), out_shape=(jax.ShapeDty...]
    unnamed x2 -> x1, local copies, waits for them, and re-layouts: 2.93 us -> 1.57 us
where the time goes in v3:
time: 85.5 us; the launch traced here: 85.2 us
  Pallas kernels  81.7 us (96%)
  local copies, waits for them, and re-layouts  2.83 us (3%)
    pallas_call x1, Pallas kernels, per_device(): pl.pallas_call(functools.partial(kernel, ns, nt), out_shape=(jax.ShapeDty...  81.7 us

profile of v3, /device:TPU:1, one launch (start us, length us, event | category | flops | bytes accessed | tf_op | source)
XLA Modules:
  0.0 85.2 jit_solution(17940028499798574200)
XLA Ops:
  0.6 81.7 %layer.1 = (bf16[32,2048]{1,0:T(8,128)(2,1)}, f32[8,128]{1,0:T(8,128)}) custom-call(s32[32]{0:T(128)} %node_lengths.1, s32[24]{0:T(128)} %group_branch.1, s32[32]{0:T(128)} %node_slot.1, s32[32]{0:T(128)} %request_group.1, f32[4,32]{1,0:T(4,128)} %bitcast.15, bf16[32,2048]{1,0:T(8,128)(2,1)} %hidden.1, f32[1,2048]{1,0:T(1,128)} %bitcast.11, ...), custom_call_target="tpu_custom_call" | custom-call | tf_op jit(solution)/shard_map/layer/pallas_call | solution.py:514
  82.4 1.3 %slice_bitcast_fusion = (f32[32]{0:T(128)}, f32[32]{0:T(128)}) fusion(f32[8,128]{1,0:T(8,128)} %get-tuple-element.6), kind=kLoop, calls=%fused_computation | loop fusion | bytes 512 | tf_op jit(solution)/shard_map/squeeze | solution.py:575
  83.6 1.6 %copy.23 = bf16[32,2048]{1,0:T(8,128)(2,1)} copy(bf16[32,2048]{1,0:T(8,128)(2,1)} %get-tuple-element.12) | data formatting | bytes 262144

commit v4 on v3

--- a/solution.py
+++ b/solution.py
@@ -75,15 +75,12 @@
     own_value,
     attn,
     inner_rows,
-    half_send1,
-    half_recv1,
-    part_send1,
-    part_recv1,
-    half_send2,
-    half_recv2,
-    part_send2,
-    part_recv2,
+    half_send,
+    half_recv,
+    part_send,
+    part_recv,
     own_sum,
+    mids,
     last_send,
     row_out,
     row_in,
@@ -174,7 +171,7 @@
             remote(buf.at[block], buf.at[block], ag_send.at[phase, nx], ag_recv.at[phase, block], tensor=sibling).wait_recv()
         for copy in copies:
             copy.wait_send()
-        return buf[...].reshape(suf, width)
+        return buf[...].reshape(nt * buf.shape[1], width)
 
     copies = gather_start(full1, 0)
 
@@ -263,13 +260,16 @@
     pair_lane = lax.broadcasted_iota(jnp.int32, (1, 128), 1)
     per_pair = 128 // (cols // heads)
     half_chunks = ns // 2
-    for pair in range(cols // 128):
-        at = slice(pair * 128, pair * 128 + 128)
-        paths = (path_root, path_kv.at[0], path_kv.at[1])
-        keys = [path[:half_chunks, :, at].reshape(cap, 128) for path in paths] + [own_key[:, at]]
-        values = [path[half_chunks:, :, at].reshape(cap, 128) for path in paths] + [own_value[:, at]]
-        for block in range(2):
-            pair_query = query[block * half : block * half + half, at]
+    block_rows = rows // 2
+
+    def attend(part_of):
+        firsts = [t * rows + part_of * block_rows for t in range(nt)]
+        for pair in range(cols // 128):
+            at = slice(pair * 128, pair * 128 + 128)
+            paths = (path_root, path_kv.at[0], path_kv.at[1])
+            keys = [path[:half_chunks, :, at].reshape(cap, 128) for path in paths] + [own_key[:, at]]
+            values = [path[half_chunks:, :, at].reshape(cap, 128) for path in paths] + [own_value[:, at]]
+            pair_query = jnp.concatenate([query[f : f + block_rows, at] for f in firsts], axis=0)
             merged = None
             for e in range(per_pair):
                 h = pair * per_pair + e
@@ -278,9 +278,13 @@
                 scores = []
                 for part in range(4):
                     score = lax.dot_general(head_query, keys[part], NT, preferred_element_type=F32)
-                    score = score + bias[h, part, :, half * (1 - block) : half * (1 - block) + suf]
+                    turned = [
+                        bias[h, part, f % half : f % half + block_rows, pl.ds(half * (1 - f // half), suf)] for f in firsts
+                    ]
+                    score = score + jnp.concatenate(turned, axis=0)
                     scores.append(score + penalty[part] if part < 3 else score)
-                peak = jnp.max(jnp.maximum(jnp.maximum(scores[0], scores[1]), jnp.maximum(scores[2], scores[3])), axis=1, keepdims=True)
+                highest = jnp.maximum(jnp.maximum(scores[0], scores[1]), jnp.maximum(scores[2], scores[3]))
+                peak = jnp.max(highest, axis=1, keepdims=True)
                 total = None
                 summed = None
                 for part in range(4):
@@ -290,9 +294,7 @@
                     summed = term if summed is None else summed + term
                 head_out = summed / jnp.sum(total, axis=1, keepdims=True)
                 merged = head_out if merged is None else jnp.where(mine, head_out, merged)
-            merged = merged.astype(BF16)
-            for r in range(half // rows):
-                attn[block * (half // rows) + r, :, at] = merged[r * rows : r * rows + rows]
+            attn[part_of, :, :, at] = merged.astype(BF16).reshape(nt, block_rows, 128)
 
     def row_send(row, phase):
         row_out[phase] = row
@@ -318,7 +320,7 @@
     is_last = me_t == nt - 1
 
     def last_projected():
-        row = dot(attn[nt - 1, rows - 16 : rows], wo[...])[15:16]
+        row = dot(attn[1, nt - 1], wo[...])[block_rows - 1 : block_rows]
         row_send(row + jnp.where(is_last, hidden[rows - 1 : rows].astype(F32), 0.0), 0)
 
     def last_inner():
@@ -403,56 +405,84 @@
 
         misc[1:2] = jnp.max(top_s[...].reshape(ns, 128), axis=0, keepdims=True)
 
-    def scatter_sum(left, weight, half_send, half_recv, part_send, part_recv, phase, early, late):
+    def sum_begin(left, weight, i):
         def product(parity):
-            picked = jnp.concatenate([left[2 * i + parity] for i in range(nx)], axis=0)
-            return dot(picked, weight[...]).reshape(nx, rows, width)
-
-        half_send[...] = product(1 - core).astype(BF16)
-        over = remote(half_send, half_recv, rs_send.at[phase, 0], rs_recv.at[phase, nx], tensor=sibling)
+            picked = jnp.concatenate([left[2 * k + parity] for k in range(nx)], axis=0)
+            return dot(picked, weight[...]).reshape(nx, block_rows, width)
+
+        half_send[i] = product(1 - core).astype(BF16)
+        over = remote(half_send.at[i], half_recv.at[i], rs_send.at[i, 0], rs_recv.at[i, nx], tensor=sibling)
         over.start()
-        own_sum[...] = product(core)
-        early()
-        over.wait_recv()
-        sent = [over]
-        for k in range(1, nx):
+        sends.append(over)
+        own_sum[i] = product(core)
+
+    others = [2, 1, 3] if nx == 4 else list(range(1, nx))
+
+    def sum_parts(i):
+        remote(half_send.at[i], half_recv.at[i], rs_send.at[i, 0], rs_recv.at[i, nx], tensor=sibling).wait_recv()
+        for k in others:
             dest = (x + k) % nx
-            part_send[k] = (own_sum[dest] + half_recv[dest].astype(F32)).astype(BF16)
+            part_send[i, k] = (own_sum[i, dest] + half_recv[i, dest].astype(F32)).astype(BF16)
             copy = remote(
-                part_send.at[k], part_recv.at[x], rs_send.at[phase, k], rs_recv.at[phase, x], tensor=dest * 2 + core
+                part_send.at[i, k], part_recv.at[i, x], rs_send.at[i, k], rs_recv.at[i, x], tensor=dest * 2 + core
             )
             copy.start()
-            sent.append(copy)
-        total = own_sum[x] + half_recv[x].astype(F32)
-        late()
-        for k in range(1, nx):
+            sends.append(copy)
+
+    def sum_end(i):
+        total = own_sum[i, x] + half_recv[i, x].astype(F32)
+        for k in others:
             source = (x + nx - k) % nx
             remote(
-                part_send.at[k], part_recv.at[source], rs_send.at[phase, k], rs_recv.at[phase, source], tensor=sibling
+                part_send.at[i, k], part_recv.at[i, source], rs_send.at[i, k], rs_recv.at[i, source], tensor=sibling
             ).wait_recv()
-            total = total + part_recv[source].astype(F32)
-        for copy in sent:
-            copy.wait_send()
+            total = total + part_recv[i, source].astype(F32)
         return total
 
+    def own_rows(part_of):
+        return pl.ds(part_of * block_rows, block_rows)
+
+    def middle(part_of):
+        total = sum_end(part_of)
+        mid = (hidden[own_rows(part_of)].astype(F32) + total).astype(BF16)
+        mids[part_of] = mid
+        full2[part_of, me_t] = rms_scale(mid.astype(F32), ff_gain[...])
+        return gather_start(full2.at[part_of], 1 + part_of)
+
+    def feed_forward(all_rows, part_of):
+        gate = dot(all_rows, wg[...])
+        up = dot(all_rows, wu[...])
+        inner = (jax.nn.gelu(gate, approximate=True) * up).astype(BF16)
+        inner_rows[part_of] = inner.reshape(nt, block_rows, inner.shape[1])
+
+    def finish(part_of):
+        out[own_rows(part_of)] = (mids[part_of].astype(F32) + sum_end(2 + part_of)).astype(BF16)
+
+    attend(1)
     for i in range(3, 8):
         loads[i].wait()
     last_projected()
-    summed = scatter_sum(attn, wo, half_send1, half_recv1, part_send1, part_recv1, 0, lambda: None, last_inner)
-    mid = (hidden[...].astype(F32) + summed).astype(BF16).astype(F32)
-    full2[me_t] = rms_scale(mid, ff_gain[...])
-    copies = gather_start(full2, 1)
+    sum_begin(attn.at[1], wo, 1)
+    attend(0)
+    sum_parts(1)
+    sum_begin(attn.at[0], wo, 0)
+    last_inner()
+    sum_parts(0)
+    copies1 = middle(1)
     last_final()
-    all_rows = gather_finish(full2, 1, copies)
+    copies0 = middle(0)
+    feed_forward(gather_finish(full2.at[1], 2, copies1), 1)
+    sum_begin(inner_rows.at[1], wd, 3)
     last_logits()
-    gate = dot(all_rows, wg[...])
-    up = dot(all_rows, wu[...])
-    inner = (jax.nn.gelu(gate, approximate=True) * up).astype(BF16)
-    inner_rows[...] = inner.reshape(nt, rows, inner.shape[1])
+    all_rows = gather_finish(full2.at[0], 1, copies0)
+    sum_parts(3)
+    feed_forward(all_rows, 0)
     top_of_words()
-    total = scatter_sum(inner_rows, wd, half_send2, half_recv2, part_send2, part_recv2, 1, top_of_group, lambda: None)
-    result = (mid + total).astype(BF16)
-    out[...] = result
+    sum_begin(inner_rows.at[0], wd, 2)
+    sum_parts(2)
+    top_of_group()
+    finish(1)
+    finish(0)
 
     top_of_all()
     for send in sends:
@@ -519,7 +549,7 @@
         scratch_shapes=[pltpu.VMEM(w.shape, BF16) for w in weights]
         + [
             pltpu.VMEM((nt, rows, width), BF16),
-            pltpu.VMEM((nt, rows, width), BF16),
+            pltpu.VMEM((2, nt, rows // 2, width), BF16),
             pltpu.VMEM((ns, chunk, cols), BF16),
             pltpu.VMEM((ns, 2, chunk, cols), BF16),
             pltpu.VMEM((ns, chunk, cols), BF16),
@@ -528,12 +558,13 @@
             pltpu.VMEM((suf, cols), BF16),
             pltpu.VMEM((suf, cols), BF16),
             pltpu.VMEM((suf, cols), BF16),
-            pltpu.VMEM((nt, rows, cols), BF16),
-            pltpu.VMEM((nt, rows, ff_down.shape[0]), BF16),
+            pltpu.VMEM((2, nt, rows // 2, cols), BF16),
+            pltpu.VMEM((2, nt, rows // 2, ff_down.shape[0]), BF16),
         ]
-        + [pltpu.VMEM((nx, rows, width), BF16) for _ in range(8)]
+        + [pltpu.VMEM((4, nx, rows // 2, width), BF16) for _ in range(4)]
         + [
-            pltpu.VMEM((nx, rows, width), F32),
+            pltpu.VMEM((4, nx, rows // 2, width), F32),
+            pltpu.VMEM((2, rows // 2, width), BF16),
             pltpu.VMEM((nt, 1, cols + 128), F32),
             pltpu.VMEM((2, 1, width), F32),
             pltpu.VMEM((2, nt, 1, width), F32),
@@ -543,10 +574,10 @@
             pltpu.VMEM((nt, 1, 128), F32),
             pltpu.VMEM((ns, 1, 128), F32),
             dma((len(weights) + 1,)),
-            dma((2, 2 * nx)),
-            dma((2, nt)),
-            dma((2, nx)),
-            dma((2, nx + 1)),
+            dma((3, 2 * nx)),
+            dma((3, nt)),
+            dma((4, nx)),
+            dma((4, nx + 1)),
             dma((4, ns)),
             dma((4, ns)),
             dma((nz,)),

time: 85.5 us -> 79.1 us (0.925)
  Pallas kernels: 81.7 us -> 75.5 us
    pallas_call x1, Pallas kernels: 81.7 us -> 75.5 us  [per_device(): pl.pallas_call(functools.partial(kernel, ns, nt), out_shape=(jax.ShapeDty...]
where the time goes in v4:
time: 79.1 us; the launch traced here: 79 us
  Pallas kernels  75.5 us (95%)
  local copies, waits for them, and re-layouts  2.83 us (4%)
    pallas_call x1, Pallas kernels, per_device(): pl.pallas_call(functools.partial(kernel, ns, nt), out_shape=(jax.ShapeDty...  75.5 us

profile of v4, /device:TPU:1, one launch (start us, length us, event | category | flops | bytes accessed | tf_op | source)
XLA Modules:
  0.0 79.0 jit_solution(5563409136843989134)
XLA Ops:
  0.6 75.5 %layer.1 = (bf16[32,2048]{1,0:T(8,128)(2,1)}, f32[8,128]{1,0:T(8,128)}) custom-call(s32[32]{0:T(128)} %node_lengths.1, s32[24]{0:T(128)} %group_branch.1, s32[32]{0:T(128)} %node_slot.1, s32[32]{0:T(128)} %request_group.1, f32[4,32]{1,0:T(4,128)} %bitcast.15, bf16[32,2048]{1,0:T(8,128)(2,1)} %hidden.1, f32[1,2048]{1,0:T(1,128)} %bitcast.11, ...), custom_call_target="tpu_custom_call" | custom-call | tf_op jit(solution)/shard_map/layer/pallas_call | solution.py:544
  76.1 1.3 %slice_bitcast_fusion = (f32[32]{0:T(128)}, f32[32]{0:T(128)}) fusion(f32[8,128]{1,0:T(8,128)} %get-tuple-element.6), kind=kLoop, calls=%fused_computation | loop fusion | bytes 512 | tf_op jit(solution)/shard_map/squeeze | solution.py:606
  77.4 1.6 %copy.23 = bf16[32,2048]{1,0:T(8,128)(2,1)} copy(bf16[32,2048]{1,0:T(8,128)(2,1)} %get-tuple-element.12) | data formatting | bytes 262144

commit v5 on v4

--- a/solution.py
+++ b/solution.py
@@ -118,6 +118,8 @@
     chunk = kv_in.shape[1]
     cap = chunk * ns // 2
 
+    sends = []
+
     def seq_peer(k):
         return ((y + k // nz) % ny) * nz + (z + k % nz) % nz
 
@@ -169,8 +171,7 @@
         for k in range(nx):
             block = ((x + nx - k) % nx) * 2 + 1 - core
             remote(buf.at[block], buf.at[block], ag_send.at[phase, nx], ag_recv.at[phase, block], tensor=sibling).wait_recv()
-        for copy in copies:
-            copy.wait_send()
+        sends.extend(copies)
         return buf[...].reshape(nt * buf.shape[1], width)
 
     copies = gather_start(full1, 0)
@@ -316,7 +317,6 @@
             row = row + row_in[phase, peer]
         return row
 
-    sends = []
     is_last = me_t == nt - 1
 
     def last_projected():
@@ -500,6 +500,12 @@
         root_z(k).wait_send()
     for k in range(1, ny):
         root_y(k).wait_send()
+
+
+def close(result, misc, out, last_rms, top_logit):
+    out[...] = result[...]
+    last_rms[...] = misc[0, : last_rms.shape[0]]
+    top_logit[...] = misc[1, : top_logit.shape[0]]
 
 
 def per_device(
@@ -603,7 +609,17 @@
         kv_chunks,
         *weights,
     )
-    return result, misc[0, :ns], misc[1, :ns]
+    return pl.pallas_call(
+        close,
+        out_shape=(
+            jax.ShapeDtypeStruct((rows, width), BF16),
+            jax.ShapeDtypeStruct((ns,), F32),
+            jax.ShapeDtypeStruct((ns,), F32),
+        ),
+        in_specs=[vmem, vmem],
+        out_specs=(vmem, vmem, vmem),
+        name="close",
+    )(result, misc)
 
 
 def solution(mesh):

time: 79.1 us -> 77 us (0.973)
  local copies, waits for them, and re-layouts: 2.83 us -> 0 us
  Pallas kernels: 75.5 us -> 76.3 us
    pallas_call x0 -> x1, Pallas kernels: none -> 1.57 us  [per_device(): pl.pallas_call(close, out_shape=(jax.ShapeDtypeStruct((rows, width), BF16...]
    unnamed x1 -> x0, local copies, waits for them, and re-layouts: 1.57 us -> none
    squeeze x1 -> x0, local copies, waits for them, and re-layouts: 1.26 us -> none  [per_device(): return (result, misc[0, :ns], misc[1, :ns])]
where the time goes in v5:
time: 77 us; the launch traced here: 76.9 us
  Pallas kernels  76.3 us (99%)
    pallas_call x1, Pallas kernels, per_device(): pl.pallas_call(functools.partial(kernel, ns, nt), out_shape=(jax.ShapeDty...  74.7 us
    pallas_call x1, Pallas kernels, per_device(): pl.pallas_call(close, out_shape=(jax.ShapeDtypeStruct((rows, width), BF16...  1.57 us

profile of v5, /device:TPU:1, one launch (start us, length us, event | category | flops | bytes accessed | tf_op | source)
XLA Modules:
  0.0 76.9 jit_solution(2249126105715892229)
XLA Ops:
  0.6 74.7 %layer.1 = (bf16[32,2048]{1,0:T(8,128)(2,1)}, f32[8,128]{1,0:T(8,128)}) custom-call(s32[32]{0:T(128)} %node_lengths.1, s32[24]{0:T(128)} %group_branch.1, s32[32]{0:T(128)} %node_slot.1, s32[32]{0:T(128)} %request_group.1, f32[4,32]{1,0:T(4,128)} %bitcast.11, bf16[32,2048]{1,0:T(8,128)(2,1)} %hidden.1, f32[1,2048]{1,0:T(1,128)} %bitcast.7, ...), custom_call_target="tpu_custom_call" | custom-call | tf_op jit(solution)/shard_map/layer/pallas_call | solution.py:550
  75.4 1.6 %close.1 = (bf16[32,2048]{1,0:T(8,128)(2,1)}, f32[32]{0:T(128)}, f32[32]{0:T(128)}) custom-call(bf16[32,2048]{1,0:T(8,128)(2,1)} %get-tuple-element.5.result, f32[8,128]{1,0:T(8,128)} %get-tuple-element.6.misc), custom_call_target="tpu_custom_call" | custom-call | tf_op jit(solution)/shard_map/close/pallas_call | solution.py:612

commit v6 on v5

--- a/solution.py
+++ b/solution.py
@@ -126,21 +126,21 @@
     def seq_from(k):
         return ((y + ny - k // nz) % ny) * nz + (z + nz - k % nz) % nz
 
+    barrier = pltpu.get_barrier_semaphore()
+
+    @pl.loop(1, ns)
+    def _(k):
+        pl.semaphore_signal(barrier, inc=1, device_id={"seq": seq_peer(k)}, device_id_type=MESH)
+
+    for k in range(1, nt):
+        pl.semaphore_signal(barrier, inc=1, device_id={"tensor": (me_t + k) % nt}, device_id_type=MESH)
+
     weights = [(wq_in, wq), (wk_in, wk), (wv_in, wv), (wo_in, wo), (wg_in, wg), (wu_in, wu), (wd_in, wd), (emb_in, emb)]
     loads = [pltpu.make_async_copy(a, b, wsem.at[i]) for i, (a, b) in enumerate(weights)]
     own_slot = pltpu.make_async_copy(kv_in.at[me_s], slots.at[me_s], wsem.at[len(weights)])
     own_slot.start()
     for load in loads:
         load.start()
-
-    barrier = pltpu.get_barrier_semaphore()
-
-    @pl.loop(1, ns)
-    def _(k):
-        pl.semaphore_signal(barrier, inc=1, device_id={"seq": seq_peer(k)}, device_id_type=MESH)
-
-    for k in range(1, nt):
-        pl.semaphore_signal(barrier, inc=1, device_id={"tensor": (me_t + k) % nt}, device_id_type=MESH)
 
     full1[me_t] = rms_scale(hidden[...].astype(F32), attn_gain[...])
     pl.semaphore_wait(barrier, ns - 1 + nt - 1)
@@ -458,6 +458,22 @@
     def finish(part_of):
         out[own_rows(part_of)] = (mids[part_of].astype(F32) + sum_end(2 + part_of)).astype(BF16)
 
+    def drain(done):
+        for send in done:
+            send.wait_send()
+
+        @pl.loop(1, ns)
+        def _(k):
+            peer = seq_peer(k)
+            remote(kv_in.at[peer], slots.at[me_s], seq_send.at[0, k], seq_recv.at[0, me_s], seq=peer).wait_send()
+            remote(kv_send.at[k], path_kv.at[:, me_s], seq_send.at[1, k], seq_recv.at[1, me_s], seq=peer).wait_send()
+            remote(last_send.at[me_t], last_all.at[me_s], seq_send.at[2, k], seq_recv.at[2, me_s], seq=peer).wait_send()
+
+        for k in range(1, nz):
+            root_z(k).wait_send()
+        for k in range(1, ny):
+            root_y(k).wait_send()
+
     attend(1)
     for i in range(3, 8):
         loads[i].wait()
@@ -479,27 +495,21 @@
     feed_forward(all_rows, 0)
     top_of_words()
     sum_begin(inner_rows.at[0], wd, 2)
+    drained = len(sends)
     sum_parts(2)
     top_of_group()
+    drain(sends[:drained])
     finish(1)
     finish(0)
 
     top_of_all()
-    for send in sends:
+    for send in sends[drained:]:
         send.wait_send()
 
     @pl.loop(1, ns)
     def _(k):
         peer = seq_peer(k)
-        remote(kv_in.at[peer], slots.at[me_s], seq_send.at[0, k], seq_recv.at[0, me_s], seq=peer).wait_send()
-        remote(kv_send.at[k], path_kv.at[:, me_s], seq_send.at[1, k], seq_recv.at[1, me_s], seq=peer).wait_send()
-        remote(last_send.at[me_t], last_all.at[me_s], seq_send.at[2, k], seq_recv.at[2, me_s], seq=peer).wait_send()
         remote(top_s.at[me_s], top_s.at[me_s], seq_send.at[3, k], seq_recv.at[3, me_s], seq=peer).wait_send()
-
-    for k in range(1, nz):
-        root_z(k).wait_send()
-    for k in range(1, ny):
-        root_y(k).wait_send()
 
 
 def close(result, misc, out, last_rms, top_logit):

time: 77 us -> 76.8 us (level)
  no operation moved by 1% of the time
where the time goes in v6:
time: 76.8 us; the launch traced here: 76.7 us
  Pallas kernels  76.1 us (99%)
    pallas_call x1, Pallas kernels, per_device(): pl.pallas_call(functools.partial(kernel, ns, nt), out_shape=(jax.ShapeDty...  74.5 us
    pallas_call x1, Pallas kernels, per_device(): pl.pallas_call(close, out_shape=(jax.ShapeDtypeStruct((rows, width), BF16...  1.57 us

profile of v6, /device:TPU:1, one launch (start us, length us, event | category | flops | bytes accessed | tf_op | source)
XLA Modules:
  0.0 76.7 jit_solution(3195745366854998669)
XLA Ops:
  0.6 74.5 %layer.1 = (bf16[32,2048]{1,0:T(8,128)(2,1)}, f32[8,128]{1,0:T(8,128)}) custom-call(s32[32]{0:T(128)} %node_lengths.1, s32[24]{0:T(128)} %group_branch.1, s32[32]{0:T(128)} %node_slot.1, s32[32]{0:T(128)} %request_group.1, f32[4,32]{1,0:T(4,128)} %bitcast.11, bf16[32,2048]{1,0:T(8,128)(2,1)} %hidden.1, f32[1,2048]{1,0:T(1,128)} %bitcast.7, ...), custom_call_target="tpu_custom_call" | custom-call | tf_op jit(solution)/shard_map/layer/pallas_call | solution.py:560
  75.1 1.6 %close.1 = (bf16[32,2048]{1,0:T(8,128)(2,1)}, f32[32]{0:T(128)}, f32[32]{0:T(128)}) custom-call(bf16[32,2048]{1,0:T(8,128)(2,1)} %get-tuple-element.5.result, f32[8,128]{1,0:T(8,128)} %get-tuple-element.6.misc), custom_call_target="tpu_custom_call" | custom-call | tf_op jit(solution)/shard_map/close/pallas_call | solution.py:622
